TPU v7x, 512 devices: a whole 4x8x8 slice. The times are simulated.
512 devices in a mesh: dom: 64 (over x, y, z_lo), col: 8 (over z_hi, core).
Axes of the slice: x: 4, y: 8, z: 8 (z_hi: 4, z_lo: 2; z = z_hi * 2 + z_lo), core: 2. Of those that a mesh axis runs over, the one named last changes fastest.
Arguments:
- inverse: bfloat16 [64, 1664, 1664], P('dom', 'col'), may hold values from -1 to 4, as said below
- trace_map: bfloat16 [64, 512, 1664], P('dom', 'col'), may hold values from -0.15625 to 0.15625
- panel_coupling: bfloat16 [64, 1664, 128], P('dom'), may hold values from -6 to 6
- coupling: float32 [64, 6, 1664], P('dom', None, 'col'), may hold values from 0.15 to 0.9
- neighbours: int32 [64, 6], P('dom'), may hold values from 0 to 63, as said below
- iface_count: int32 [64], replicated, may hold values from 26 to 104, as said below
- surface_rows: int32 [64, 8, 1, 64], P('dom', 'col'), may hold values from 0 to 63
- factor: float32 [32768, 2048], P(('dom', 'col')), may hold values from -2 to 2
- colloc: float32 [3, 32768], P(None, ('dom', 'col')), may hold values from -1 to 1
- quad_points: float32 [3, 4, 32768], P(None, None, ('dom', 'col')), may hold values from -1 to 1
- quad_weight: float32 [4, 32768], P(None, ('dom', 'col')), may hold values from 2 to 16
- panel_block: int32 [2], replicated, may hold values from 0 to 511
Outputs:
- panel_columns: float32 [32768, 128], P(('dom', 'col'))
Inputs may be any that keep to these rules, and one draw needn't show every extreme that they name: Each domain's inverse is symmetric. `neighbours`: each domain lists 6 different domains, never itself. `iface_count`: some domain has exactly 104.
All inputs are finite; a program needn't handle non-finite values.
Results may differ from a plain program's by a relative error of at most 0.007.
Values may be sent and summed in bfloat16 or wider, within the bound.
No kernel may reach another device: no remote copies, remote signals or barrier semaphores. Data moves between devices by JAX's collectives and lax.ppermute only.
A program may use at most 64 MiB of HBM per device.

v0:
```python
import math
import jax
import jax.numpy as jnp
from jax import lax
from jax.sharding import PartitionSpec as P

MB = 208
P_SIZE = 64
NPAN = 2
SLOTS = 1
WAVE_NUMBER = 8.0
SMOOTHING = 0.05


def broadcast(block, axis, source):
    block = jnp.where(lax.axis_index(axis) == source, block, jnp.zeros_like(block))
    return lax.psum(block, axis)


def local(
    inverse,
    trace_map,
    panel_coupling,
    coupling,
    neighbours,
    iface_count,
    surface_rows,
    factor,
    colloc,
    quad_points,
    quad_weight,
    panel_block,
):
    dom_index = lax.axis_index("dom")
    col_index = lax.axis_index("col")
    domain_count = lax.axis_size("dom")
    inverse_rows = inverse[0]
    block_rows = inverse_rows.shape[0]
    panel_loads = panel_coupling[0]
    column_count = panel_loads.shape[1]
    first_row = col_index * block_rows
    own_loads = lax.dynamic_slice_in_dim(panel_loads, first_row, block_rows, 0)
    row_numbers = first_row + jnp.arange(block_rows, dtype=jnp.int32)
    own_count = iface_count[dom_index]
    live_rows = (row_numbers % MB < own_count).astype(jnp.float32)[:, None]
    first_apply = jnp.dot(inverse_rows, panel_loads, preferred_element_type=jnp.float32)
    first_values = (first_apply * live_rows).astype(jnp.bfloat16)
    weights_here = coupling[0]
    listed = neighbours[0]
    shards = lax.all_gather(first_values[None], "dom", axis=0, tiled=True)
    count_here = shards.shape[0]
    matches = (listed[:, None] == jnp.arange(count_here, dtype=jnp.int32)[None, :]).astype(
        jnp.float32
    )
    factors = jnp.einsum("ke,kr->er", matches, weights_here)
    correction = jnp.sum(factors[:, :, None] * shards, axis=0)
    loaded = (own_loads.astype(jnp.float32) - live_rows * correction).astype(jnp.bfloat16)
    map_rows = trace_map[0]
    columns = inverse_rows
    second_rows = jnp.dot(
        columns,
        lax.all_gather(loaded, "col", axis=0, tiled=True),
        preferred_element_type=jnp.float32,
    ).astype(jnp.bfloat16)
    columns = map_rows
    traces = jnp.dot(
        columns,
        lax.all_gather(second_rows, "col", axis=0, tiled=True),
        preferred_element_type=jnp.float32,
    )
    traces = traces.astype(jnp.bfloat16).reshape(SLOTS, domain_count, column_count)
    arrived = lax.all_to_all(traces, "dom", split_axis=1, concat_axis=1, tiled=True)
    row_slots = surface_rows[0, 0].reshape(-1)
    factor_rows = factor.shape[0]
    surface_sum = (
        jnp.zeros((factor_rows, column_count), jnp.float32)
        .at[row_slots]
        .add(arrived.reshape(-1, column_count).astype(jnp.float32))
    )
    factor_list = []
    points_list = []
    weights_list = []
    for panel_number in range(NPAN):
        begin_row = panel_block[panel_number] * P_SIZE
        owner_device = begin_row // factor_rows
        received = (
            broadcast(factor, ("dom", "col"), owner_device),
            broadcast(quad_points, ("dom", "col"), owner_device),
            broadcast(quad_weight, ("dom", "col"), owner_device),
        )
        factor_list.append(received[0])
        points_list.append(received[1])
        weights_list.append(received[2])
    panel_factor = jnp.concatenate(factor_list, axis=0)
    panel_points = jnp.concatenate(points_list, axis=2)
    panel_weights = jnp.concatenate(weights_list, axis=1)
    shifted = colloc[:, :, None, None] - panel_points[:, None, :, :]
    squared = jnp.sum(shifted * shifted, axis=0)
    green_values = jnp.cos(WAVE_NUMBER * jnp.sqrt(squared)) / (
        4.0 * math.pi * jnp.sqrt(squared + SMOOTHING * SMOOTHING)
    )
    kernel_block = jnp.sum(panel_weights[None, :, :] * green_values, axis=1)
    prior_update = lax.dot_general(
        factor,
        panel_factor,
        (((1,), (1,)), ((), ())),
        precision=lax.Precision.HIGHEST,
        preferred_element_type=jnp.float32,
    )
    return kernel_block - surface_sum - prior_update


def solution(mesh):
    in_specs = (
        P("dom", "col", None),
        P("dom", "col", None),
        P("dom", None, None),
        P("dom", None, "col"),
        P("dom", None),
        P(),
        P("dom", "col", None, None),
        P(("dom", "col"), None),
        P(None, ("dom", "col")),
        P(None, None, ("dom", "col")),
        P(None, ("dom", "col")),
        P(),
    )
    out_specs = P(("dom", "col"), None)
    return jax.shard_map(local, mesh=mesh, in_specs=in_specs, out_specs=out_specs, check_vma=False)
```

profile of v0, /device:TPU:1, one launch (start us, length us, event | category | flops | bytes accessed | tf_op | source)
XLA Modules:
  0.0 388.6 jit_solution(3497062849710801463)
XLA Ops:
  7.4 0.0 copy-start
  7.4 0.0 copy-start.8
  7.4 0.0 copy-start.6
  7.4 0.0 copy-start.3
  7.4 0.0 copy-start.7
  7.4 0.0 copy-start.4
  7.4 0.0 copy-start.5
  7.4 0.0 all-gather.3.cloned.1.call-start
  7.5 1.3 dynamic_slice.7
  8.7 0.7 compare_convert_fusion
  9.4 0.0 copy-done
  9.4 2.0 fusion.1
  11.4 0.0 all-gather.3.cloned.1.call-update
  11.4 0.0 all-reduce.4.cloned.1.call-start
  11.5 1.3 fusion.24
  14.1 2.1 broadcast_select_fusion.1
  16.3 0.0 copy-start.2
  16.3 0.0 all-reduce.4.cloned.1.call-update
  16.3 0.0 copy-done.8
  16.3 0.0 copy-done.6
  16.3 0.0 copy-done.3
  16.4 108.0 %all-reduce = (f32[3,4,64]{2,1,0:T(4,128)S(1)}, f32[3,4,64]{2,1,0:T(4,128)S(1)}, f32[4,64]{1,0:T(4,128)S(1)}, f32[4,64]{1,0:T(4,128)S(1)}) all-reduce(f32[3,4,64]{2,1,0:T(4,128)S(1)} %get-tuple-element.14, f32[3,4,64]{2,1,0:T(4,128)S(1)} %get-tuple-element.13, ...), channel_id=1, replica_groups=mesh['dom'=64,'col'=8] {'dom','col'}, use_global_device_ids=true, to_apply=%region_3.4 | all-reduce | flops 2048 | bytes 16384 | tf_op jit(solution)/shard_map/psum | solution.py:17
  124.3 0.1 pad_maximum_fusion
  124.4 0.1 pad_maximum_fusion.1
  124.5 0.0 copy-done.7
  124.5 0.0 copy-done.4
  124.5 0.3 fusion.18
  124.8 0.0 copy-done.5
  124.8 0.1 multiply_reduce_fusion
  124.9 149.1 %all-gather.3.cloned.1.call-done = bf16[13312,128]{1,0:T(8,128)(2,1)} async-done(((bf16[208,128]{1,0:T(8,128)(2,1)}), bf16[13312,128]{1,0:T(8,128)(2,1)}) %all-gather.3.cloned.1.call-update) | async-done | bytes 3407888 | tf_op jit(solution)/shard_map/all_gather | solution.py:50
  274.0 0.0 copy-start.1
  274.0 4.0 %fusion = f32[208,128]{1,0:T(8,128)S(1)} fusion(bf16[64,208,128]{2,1,0:T(8,128)(2,1)} %bitcast.46, f32[64,208]{1,0:T(8,128)S(1)} %fusion.18), kind=kLoop, calls=%fused_computation.2 | loop fusion | flops 5085184 | bytes 3567616 | tf_op jit(solution)/shard_map/reduce_sum | solution.py:56
  278.1 0.9 fusion.12
  279.0 66.1 %all_gather.10 = bf16[1664,128]{1,0:T(8,128)(2,1)S(1)} all-gather(bf16[208,128]{1,0:T(8,128)(2,1)S(1)} %fusion.12), channel_id=1, replica_groups=mesh['dom'=64,'col'=8] {'col'}, dimensions={0}, use_global_device_ids=true | all-gather | bytes 479232 | tf_op jit(solution)/shard_map/all_gather | solution.py:62
  345.1 0.4 fusion.2
  345.4 14.9 %all_gather.11 = bf16[1664,128]{1,0:T(8,128)(2,1)S(1)} all-gather(bf16[208,128]{1,0:T(8,128)(2,1)S(1)} %fusion.2), channel_id=1, replica_groups=mesh['dom'=64,'col'=8] {'col'}, dimensions={0}, use_global_device_ids=true | all-gather | bytes 479232 | tf_op jit(solution)/shard_map/all_gather | solution.py:68
  360.4 0.0 copy-done.2
  360.4 0.2 fusion.4
  360.6 0.6 copy.15
  361.2 6.8 %all-to-all-start = ((bf16[1,64,128]{2,0,1:T(2,128)(2,1)}), bf16[1,64,128]{2,0,1:T(2,128)(2,1)S(1)}, u32[]{:S(2)}, u32[]{:S(2)}) async-start(bf16[1,64,128]{2,0,1:T(2,128)(2,1)} %copy.15), calls=%async_computation | async-start | bytes 65536 | tf_op jit(solution)/shard_map/all_to_all | solution.py:72
  368.0 0.5 multiply_reduce_fusion.1
  368.6 8.7 %all-to-all-done = bf16[1,64,128]{2,0,1:T(2,128)(2,1)S(1)} async-done(((bf16[1,64,128]{2,0,1:T(2,128)(2,1)}), bf16[1,64,128]{2,0,1:T(2,128)(2,1)S(1)}, u32[]{:S(2)}, u32[]{:S(2)}) %all-to-all-start) | async-done | bytes 16416 | tf_op jit(solution)/shard_map/all_to_all | solution.py:72
  377.2 0.8 scatter_custom_fusion
  378.1 0.0 all-reduce.4.cloned.1.call-done
  378.1 0.0 copy-done.1
  378.1 3.0 fusion.3
  (3 shorter events, 0.0 us)
Async XLA Ops:
  7.4 2.0 copy-start
  7.4 8.9 %copy-start.8 = (s32[1,1,1,64]{3,2,1,0:T(1,128)S(1)}, s32[1,1,1,64]{3,2,1,0:T(1,128)}, u32[]{:S(2)}) copy-start(s32[1,1,1,64]{3,2,1,0:T(1,128)} %param.18) | copy-start | bytes 772
  7.4 9.0 %copy-start.6 = (f32[4,64]{1,0:T(4,128)S(1)}, f32[4,64]{1,0:T(4,128)}, u32[]{:S(2)}) copy-start(f32[4,64]{1,0:T(4,128)} %param.22) | copy-start | bytes 3076
  7.4 9.0 %copy-start.3 = (f32[3,4,64]{2,1,0:T(4,128)S(1)}, f32[3,4,64]{2,1,0:T(4,128)}, u32[]{:S(2)}) copy-start(f32[3,4,64]{2,1,0:T(4,128)} %param.21) | copy-start | bytes 9220
  7.4 117.1 %copy-start.7 = (s32[1,6]{1,0:T(1,128)S(1)}, s32[1,6]{1,0:T(1,128)}, u32[]{:S(2)}) copy-start(s32[1,6]{1,0:T(1,128)} %param.16) | copy-start | bytes 76
  7.4 117.1 %copy-start.4 = (f32[1,6,208]{2,0,1:T(1,128)S(1)}, f32[1,6,208]{2,0,1:T(1,128)}, u32[]{:S(2)}) copy-start(f32[1,6,208]{2,0,1:T(1,128)} %param.15) | copy-start | bytes 14980
  7.4 117.4 %copy-start.5 = (f32[3,64]{1,0:T(4,128)S(1)}, f32[3,64]{1,0:T(4,128)}, u32[]{:S(2)}) copy-start(f32[3,64]{1,0:T(4,128)} %param.20) | copy-start | bytes 2308
  7.4 266.6 %all-gather.3.cloned.1.call-start = ((), (), s32[]{:S(2)}) async-start(), calls=%async_computation.1 | async-start | bytes 3461120 | tf_op jit(solution)/shard_map/all_gather | solution.py:50
  11.4 366.7 %all-reduce.4.cloned.1.call-start = ((), (), s32[]{:S(2)}) async-start(), calls=%async_computation.2 | async-start | bytes 2097152 | tf_op jit(solution)/shard_map/psum | solution.py:17
  16.3 344.1 %copy-start.2 = (bf16[1,64,1664]{2,1,0:T(8,128)(2,1)S(1)}, bf16[1,64,1664]{2,1,0:T(8,128)(2,1)}, u32[]{:S(2)}) copy-start(bf16[1,64,1664]{2,1,0:T(8,128)(2,1)} %param.13) | copy-start | bytes 638980
  274.0 104.1 %copy-start.1 = (f32[64,2048]{1,0:T(8,128)S(1)}, f32[64,2048]{1,0:T(8,128)}, u32[]{:S(2)}) copy-start(f32[64,2048]{1,0:T(8,128)} %param.19) | copy-start | bytes 1572868
  361.2 16.0 %all-to-all-start = ((bf16[1,64,128]{2,0,1:T(2,128)(2,1)}), bf16[1,64,128]{2,0,1:T(2,128)(2,1)S(1)}, u32[]{:S(2)}, u32[]{:S(2)}) async-start(bf16[1,64,128]{2,0,1:T(2,128)(2,1)} %copy.15), calls=%async_computation | async-start | bytes 65536 | tf_op jit(solution)/shard_map/all_to_all | solution.py:72
Sparse Core Ops, SparseCore 0:
  11.6 262.4 all-gather.2
Sparse Core Ops, SparseCore 1:
  17.2 283.3 all-reduce.3
where the time goes:
time: 389 us
  blocking collectives  189 us (49%)
  waiting for transfers between devices  158 us (41%)
  between operations  16.3 us (4%)
  other arithmetic  9.37 us (2%)
  starting transfers between devices  6.86 us (2%)
  matrix products  5.84 us (2%)
    all_gather x1, waiting for transfers between devices, local(): shards = lax.all_gather(first_values[None], 'dom', axis=0, tiled=True)  149 us
    psum x1, blocking collectives, broadcast(): return lax.psum(block, axis)  108 us
    all_gather x1, blocking collectives, local(): lax.all_gather(loaded, 'col', axis=0, tiled=True)  66.1 us
    all_gather x1, blocking collectives, local(): lax.all_gather(second_rows, 'col', axis=0, tiled=True)  14.9 us
    all_to_all x1, waiting for transfers between devices, local(): lax.all_to_all(traces, 'dom', split_axis=1, concat_axis=1, tiled=True)  8.67 us
  transfers between devices with their start and end apart: 3, of which 2 were waited for; matrix products, arithmetic and copies ran while one was open for 3% of the time, Pallas kernels for 0%

commit v1 on v0

--- a/solution.py
+++ b/solution.py
@@ -59,7 +59,9 @@
     columns = inverse_rows
     second_rows = jnp.dot(
         columns,
-        lax.all_gather(loaded, "col", axis=0, tiled=True),
+        jnp.concatenate(
+            lax.all_to_all(jnp.stack([loaded] * lax.axis_size("col")), "col", 0, 0), axis=0
+        ),
         preferred_element_type=jnp.float32,
     ).astype(jnp.bfloat16)
     columns = map_rows

time: 389 us -> 480 us (1.23)
  waiting for transfers between devices: 158 us -> 266 us
  blocking collectives: 189 us -> 116 us
  starting transfers between devices: 6.86 us -> 61.5 us
    all_gather x1, waiting for transfers between devices: 149 us -> 257 us  [local(): shards = lax.all_gather(first_values[None], 'dom', axis=0, tiled=True)]
    all_gather x1 -> x0, blocking collectives: 66.1 us -> none  [local(): lax.all_gather(loaded, 'col', axis=0, tiled=True)]
    all_to_all x0 -> x1, starting transfers between devices: none -> 55 us  [local(): lax.all_to_all(jnp.stack([loaded] * lax.axis_size('col')), 'col', 0, 0)]
    psum x1, blocking collectives: 108 us -> 100 us  [broadcast(): return lax.psum(block, axis)]
  transfers between devices with their start and end apart: 3 -> 4, of which waited for: 2 -> 2; matrix products, arithmetic and copies ran while one was open for 3% -> 3% of each run, Pallas kernels for 0% -> 0%
where the time goes in v1:
time: 480 us; the launch traced here: 479 us
  waiting for transfers between devices  266 us (55%)
  blocking collectives  116 us (24%)
  starting transfers between devices  61.5 us (13%)
  between operations  16.3 us (3%)
  other arithmetic  9.39 us (2%)
  matrix products  5.83 us (1%)
    all_gather x1, waiting for transfers between devices, local(): shards = lax.all_gather(first_values[None], 'dom', axis=0, tiled=True)  257 us
    psum x1, blocking collectives, broadcast(): return lax.psum(block, axis)  100 us
    all_to_all x1, starting transfers between devices, local(): lax.all_to_all(jnp.stack([loaded] * lax.axis_size('col')), 'col', 0, 0)  55 us
    all_gather x1, blocking collectives, local(): lax.all_gather(second_rows, 'col', axis=0, tiled=True)  16.3 us
  transfers between devices with their start and end apart: 4, of which 2 were waited for; matrix products, arithmetic and copies ran while one was open for 3% of the time, Pallas kernels for 0%

profile of v1, /device:TPU:1, one launch (start us, length us, event | category | flops | bytes accessed | tf_op | source)
XLA Modules:
  0.0 479.5 jit_solution(17202009842234084114)
XLA Ops:
  7.4 0.0 copy-start
  7.4 0.0 copy-start.3
  7.4 0.0 copy-start.7
  7.4 0.0 copy-start.4
  7.4 0.0 all-gather.3.cloned.1.call-start
  7.4 1.3 dynamic_slice.7
  8.7 0.7 compare_convert_fusion
  9.4 0.0 copy-done
  9.4 2.0 fusion.1
  11.4 0.0 all-gather.3.cloned.1.call-update
  11.4 0.0 all-reduce.4.cloned.1.call-start
  11.4 1.3 fusion.26
  14.0 2.2 broadcast_select_fusion.1
  16.2 0.0 copy-start.6
  16.2 0.0 copy-start.5
  16.2 0.0 copy-start.8
  16.2 0.0 all-reduce.4.cloned.1.call-update
  16.2 0.0 copy-done.3
  16.2 0.0 copy-done.7
  16.2 0.0 copy-done.4
  16.2 0.3 fusion.20
  16.5 257.4 %all-gather.3.cloned.1.call-done = bf16[13312,128]{1,0:T(8,128)(2,1)} async-done(((bf16[208,128]{1,0:T(8,128)(2,1)}), bf16[13312,128]{1,0:T(8,128)(2,1)}) %all-gather.3.cloned.1.call-update) | async-done | bytes 3407888 | tf_op jit(solution)/shard_map/all_gather | solution.py:50
  273.9 0.0 copy-start.2
  273.9 0.0 copy-start.1
  273.9 4.0 fusion
  277.9 0.9 fusion.14
  278.8 0.8 stack.5
  279.7 55.0 %all-to-all-start = ((bf16[8,208,128]{2,1,0:T(8,128)(2,1)}), bf16[8,208,128]{2,1,0:T(8,128)(2,1)S(1)}, u32[]{:S(2)}, u32[]{:S(2)}) async-start(bf16[8,208,128]{2,1,0:T(8,128)(2,1)} %stack.5), calls=%async_computation | async-start | bytes 851968 | tf_op jit(solution)/shard_map/all_to_all | solution.py:63
  334.7 0.0 copy-done.6
  334.7 100.0 %all-reduce = (f32[3,4,64]{2,1,0:T(4,128)S(1)}, f32[3,4,64]{2,1,0:T(4,128)S(1)}, f32[4,64]{1,0:T(4,128)S(1)}, f32[4,64]{1,0:T(4,128)S(1)}) all-reduce(f32[3,4,64]{2,1,0:T(4,128)S(1)} %get-tuple-element.14, f32[3,4,64]{2,1,0:T(4,128)S(1)} %get-tuple-element.13, ...), channel_id=1, replica_groups=mesh['dom'=64,'col'=8] {'dom','col'}, use_global_device_ids=true, to_apply=%region_3.4 | all-reduce | flops 2048 | bytes 16384 | tf_op jit(solution)/shard_map/psum | solution.py:17
  434.7 0.1 pad_maximum_fusion.1
  434.8 0.1 pad_maximum_fusion
  434.8 0.0 copy-done.5
  434.8 0.1 multiply_reduce_fusion
  435.0 0.0 copy-done.8
  435.0 0.0 all-to-all-done
  435.0 0.4 fusion.2
  435.4 16.3 %all_gather.7 = bf16[1664,128]{1,0:T(8,128)(2,1)S(1)} all-gather(bf16[208,128]{1,0:T(8,128)(2,1)S(1)} %fusion.2), channel_id=1, replica_groups=mesh['dom'=64,'col'=8] {'col'}, dimensions={0}, use_global_device_ids=true | all-gather | bytes 479232 | tf_op jit(solution)/shard_map/all_gather | solution.py:70
  451.7 0.0 copy-done.2
  451.7 0.2 fusion.4
  451.9 0.6 copy.15
  452.5 6.4 %all-to-all-start.1 = ((bf16[1,64,128]{2,0,1:T(2,128)(2,1)}), bf16[1,64,128]{2,0,1:T(2,128)(2,1)S(1)}, u32[]{:S(2)}, u32[]{:S(2)}) async-start(bf16[1,64,128]{2,0,1:T(2,128)(2,1)} %copy.15), calls=%async_computation.1 | async-start | bytes 65536 | tf_op jit(solution)/shard_map/all_to_all | solution.py:74
  458.9 0.5 multiply_reduce_fusion.1
  459.5 8.7 %all-to-all-done.1 = bf16[1,64,128]{2,0,1:T(2,128)(2,1)S(1)} async-done(((bf16[1,64,128]{2,0,1:T(2,128)(2,1)}), bf16[1,64,128]{2,0,1:T(2,128)(2,1)S(1)}, u32[]{:S(2)}, u32[]{:S(2)}) %all-to-all-start.1) | async-done | bytes 16416 | tf_op jit(solution)/shard_map/all_to_all | solution.py:74
  468.2 0.8 scatter_custom_fusion
  469.0 0.0 all-reduce.4.cloned.1.call-done
  469.0 0.0 copy-done.1
  469.0 3.0 fusion.3
  (3 shorter events, 0.0 us)
Async XLA Ops:
  7.4 2.0 copy-start
  7.4 8.8 %copy-start.3 = (f32[3,4,64]{2,1,0:T(4,128)S(1)}, f32[3,4,64]{2,1,0:T(4,128)}, u32[]{:S(2)}) copy-start(f32[3,4,64]{2,1,0:T(4,128)} %param.21) | copy-start | bytes 9220
  7.4 8.9 %copy-start.7 = (s32[1,6]{1,0:T(1,128)S(1)}, s32[1,6]{1,0:T(1,128)}, u32[]{:S(2)}) copy-start(s32[1,6]{1,0:T(1,128)} %param.16) | copy-start | bytes 76
  7.4 8.9 %copy-start.4 = (f32[1,6,208]{2,0,1:T(1,128)S(1)}, f32[1,6,208]{2,0,1:T(1,128)}, u32[]{:S(2)}) copy-start(f32[1,6,208]{2,0,1:T(1,128)} %param.15) | copy-start | bytes 14980
  7.4 266.5 %all-gather.3.cloned.1.call-start = ((), (), s32[]{:S(2)}) async-start(), calls=%async_computation.2 | async-start | bytes 3461120 | tf_op jit(solution)/shard_map/all_gather | solution.py:50
  11.4 457.6 %all-reduce.4.cloned.1.call-start = ((), (), s32[]{:S(2)}) async-start(), calls=%async_computation.3 | async-start | bytes 2097152 | tf_op jit(solution)/shard_map/psum | solution.py:17
  16.2 318.5 %copy-start.6 = (f32[4,64]{1,0:T(4,128)S(1)}, f32[4,64]{1,0:T(4,128)}, u32[]{:S(2)}) copy-start(f32[4,64]{1,0:T(4,128)} %param.22) | copy-start | bytes 3076
  16.2 418.7 %copy-start.5 = (f32[3,64]{1,0:T(4,128)S(1)}, f32[3,64]{1,0:T(4,128)}, u32[]{:S(2)}) copy-start(f32[3,64]{1,0:T(4,128)} %param.20) | copy-start | bytes 2308
  16.2 418.8 %copy-start.8 = (s32[1,1,1,64]{3,2,1,0:T(1,128)S(1)}, s32[1,1,1,64]{3,2,1,0:T(1,128)}, u32[]{:S(2)}) copy-start(s32[1,1,1,64]{3,2,1,0:T(1,128)} %param.18) | copy-start | bytes 772
  273.9 177.8 %copy-start.2 = (bf16[1,64,1664]{2,1,0:T(8,128)(2,1)S(1)}, bf16[1,64,1664]{2,1,0:T(8,128)(2,1)}, u32[]{:S(2)}) copy-start(bf16[1,64,1664]{2,1,0:T(8,128)(2,1)} %param.13) | copy-start | bytes 638980
  273.9 195.1 %copy-start.1 = (f32[64,2048]{1,0:T(8,128)S(1)}, f32[64,2048]{1,0:T(8,128)}, u32[]{:S(2)}) copy-start(f32[64,2048]{1,0:T(8,128)} %param.19) | copy-start | bytes 1572868
  279.7 155.3 %all-to-all-start = ((bf16[8,208,128]{2,1,0:T(8,128)(2,1)}), bf16[8,208,128]{2,1,0:T(8,128)(2,1)S(1)}, u32[]{:S(2)}, u32[]{:S(2)}) async-start(bf16[8,208,128]{2,1,0:T(8,128)(2,1)} %stack.5), calls=%async_computation | async-start | bytes 851968 | tf_op jit(solution)/shard_map/all_to_all | solution.py:63
  452.5 15.6 %all-to-all-start.1 = ((bf16[1,64,128]{2,0,1:T(2,128)(2,1)}), bf16[1,64,128]{2,0,1:T(2,128)(2,1)S(1)}, u32[]{:S(2)}, u32[]{:S(2)}) async-start(bf16[1,64,128]{2,0,1:T(2,128)(2,1)} %copy.15), calls=%async_computation.1 | async-start | bytes 65536 | tf_op jit(solution)/shard_map/all_to_all | solution.py:74
Sparse Core Ops, SparseCore 0:
  11.5 262.3 all-gather.2
Sparse Core Ops, SparseCore 1:
  17.1 283.1 all-reduce.3
